TPU v7x, 32 devices: a whole 2x2x4 slice. The times are simulated.
32 devices in a mesh: context: 8 (over z, x), tensor: 4 (over y, core).
Axes of the slice: x: 2, y: 2, z: 4, core: 2. Of those that a mesh axis runs over, the one named last changes fastest.
Arguments:
- queries: bfloat16 [1024, 4096], P('context', 'tensor'), may hold values from -6 to 6
- key_vectors: bfloat16 [1024, 4096], P('context', 'tensor'), may hold values from -6 to 6
- value_vectors: bfloat16 [1024, 4096], P('context', 'tensor'), may hold values from -6 to 6
- doc_lengths: int32 [16], replicated, may hold values from 1 to 256, 1024 in all
- head_gain: float32 [4096], P('tensor'), may hold values from 0.5 to 1.5
- output_weight: bfloat16 [4096, 6144], P('tensor'), may hold values from -0.125 to 0.125
- residual: bfloat16 [1024, 6144], P('context', 'tensor'), may hold values from -6 to 6
- final_gain: float32 [6144], replicated, may hold values from 0.5 to 1.5
Outputs:
- next_stream: bfloat16 [1024, 6144], P('context', 'tensor')
- normed: bfloat16 [1024, 6144], P('context')
Inputs may be any that keep to these rules, and one draw needn't show every extreme that they name: `doc_lengths`: the 16 lengths sum to 1024, and one of them equals 256.
All inputs are finite; a program needn't handle non-finite values.
Results may differ from a plain program's by a relative error of at most 0.017.
Values may be sent and summed in bfloat16 or wider, within the bound.
A program may use at most 64 MiB of HBM per device.

v0:
```python
import jax
import jax.numpy as jnp
from jax import lax
from jax.sharding import PartitionSpec as P

HEAD = 128


EPSILON = 1e-06


def entering(shard, axis, join, neutral):
    place = lax.axis_index(axis)
    gathered = jax.tree.map(
        lambda a, kind: lax.all_gather(a.astype(kind), axis), shard, (jnp.bfloat16, jnp.bfloat16)
    )
    state = jax.tree.map(lambda a, e: jnp.zeros_like(a) + jnp.asarray(e, a.dtype), shard, neutral)

    def one(step, state):
        return join(
            state,
            jax.tree.map(
                lambda a, own: lax.dynamic_index_in_dim(a, step, 0, False).astype(own.dtype),
                gathered,
                shard,
            ),
        )

    return lax.fori_loop(0, place, one, state)


def doc_index(positions, starts):
    return jnp.sum((positions[:, None] >= starts[None, :]).astype(jnp.int32), axis=1) - 1


def row_norm(rows, gain):
    squares = jnp.mean(rows * rows, axis=-1, keepdims=True)
    return rows * lax.rsqrt(squares + EPSILON) * gain


def combine_states(earlier, later):
    return (
        jnp.maximum(earlier[0], later[0]),
        jnp.where(later[0] > 0.5, later[1], earlier[1] + later[1]),
    )


def local(
    queries, key_vectors, value_vectors, doc_lengths, head_gain, output_weight, residual, final_gain
):
    tok_count = queries.shape[0]
    head_count = queries.shape[1] // HEAD
    starts = jnp.cumsum(doc_lengths) - doc_lengths
    first_pos = lax.axis_index("context") * tok_count
    positions = first_pos + jnp.arange(tok_count, dtype=jnp.int32)
    doc_ids = doc_index(positions, starts)
    prev_doc = doc_index(jnp.reshape(first_pos - 1, (1,)), starts)[0]
    carry_mask = doc_ids == prev_doc
    last_mask = doc_ids == doc_ids[-1]
    reset_flag = (doc_ids[-1] != prev_doc).astype(jnp.float32)
    query_heads = queries.reshape(tok_count, head_count, HEAD)
    key_heads = key_vectors.reshape(tok_count, head_count, HEAD)
    value_heads = value_vectors.reshape(tok_count, head_count, HEAD)
    masked_keys = jnp.where(last_mask[:, None, None], key_heads, jnp.zeros_like(key_heads))
    local_state = jnp.einsum(
        "thd,the->hde", masked_keys, value_heads, preferred_element_type=jnp.float32
    )
    identity = (jnp.zeros((), jnp.float32), jnp.zeros_like(local_state))
    incoming = entering((reset_flag, local_state), "context", combine_states, identity)
    scores = jnp.einsum("thd,shd->hts", query_heads, key_heads, preferred_element_type=jnp.float32)
    causal_mask = (positions[None, :] <= positions[:, None]) & (
        doc_ids[:, None] == doc_ids[None, :]
    )
    weights = jnp.where(causal_mask[None], scores, 0.0).astype(jnp.bfloat16)
    inner_term = jnp.einsum(
        "hts,shd->thd", weights, value_heads, preferred_element_type=jnp.float32
    )
    cross_term = jnp.einsum(
        "thd,hde->the",
        query_heads,
        incoming[1].astype(jnp.bfloat16),
        preferred_element_type=jnp.float32,
    )
    attention = inner_term + jnp.where(carry_mask[:, None, None], cross_term, 0.0)
    head_out = (
        row_norm(attention, head_gain.reshape(head_count, HEAD))
        .astype(jnp.bfloat16)
        .reshape(tok_count, head_count * HEAD)
    )
    summed_rows = lax.psum_scatter(
        jnp.dot(head_out, output_weight, preferred_element_type=jnp.float32).astype(jnp.bfloat16),
        "tensor",
        scatter_dimension=0,
        tiled=True,
    ).astype(jnp.float32)
    stream_rows = lax.all_to_all(residual, "tensor", split_axis=0, concat_axis=1, tiled=True)
    hidden_rows = (stream_rows.astype(jnp.float32) + summed_rows).astype(jnp.bfloat16)
    normed_part = row_norm(hidden_rows.astype(jnp.float32), final_gain).astype(jnp.bfloat16)
    normed = lax.all_gather(normed_part, "tensor", axis=0, tiled=True)
    next_stream = lax.all_to_all(hidden_rows, "tensor", split_axis=1, concat_axis=0, tiled=True)
    return (next_stream, normed)


def solution(mesh):
    placed = (
        P("context", "tensor"),
        P("context", "tensor"),
        P("context", "tensor"),
        P(),
        P("tensor"),
        P("tensor", None),
        P("context", "tensor"),
        P(),
    )
    return jax.shard_map(
        local,
        mesh=mesh,
        in_specs=placed,
        out_specs=(P("context", "tensor"), P("context", None)),
        check_vma=False,
    )
```

profile of v0, /device:TPU:11, one launch (start us, length us, event | category | flops | bytes accessed | tf_op | source)
XLA Modules:
  0.0 149.0 jit_solution(10763485002070784579)
XLA Ops:
  7.2 0.0 copy-start
  7.2 0.0 all-gather.6.cloned.1.call-start
  7.2 0.7 copy.37
  8.0 0.1 reduce.2
  8.1 1.3 fusion.22
  9.4 0.1 convert_reduce_fusion
  9.5 0.6 slice.4
  10.8 1.1 copy.47
  11.9 0.6 broadcast_compare_fusion.1
  12.5 1.9 %convolution_convert_fusion.1 = bf16[8,128,128]{2,1,0:T(8,128)(2,1)} fusion(bf16[128,8,128]{0,2,1:T(8,128)(2,1)S(1)} %bitcast.70, pred[128]{0:T(512)(128)(4,1)S(1)} %get-tuple-element.62, bf16[128,1024]{1,0:T(8,128)(2,1)} %param.12), kind=kOutput, calls=%fused_computation.8 | convolution fusion | flops 33816576 | bytes 786560 | tf_op jit(solution)/shard_map/thd,the->hde/dot_general | solution.py:65
  14.4 0.0 all-gather.6.cloned.1.call-update
  14.4 0.0 reduce-scatter.2.cloned.1.call-start
  15.1 1.3 dynamic-slice
  16.4 0.7 dynamic-update-slice
  17.1 12.1 %all-reduce = bf16[8]{0:T(256)(128)(2,1)S(1)} all-reduce(bf16[8]{0:T(256)(128)(2,1)S(1)} %dynamic-update-slice), channel_id=1, replica_groups=mesh['context'=8,'tensor'=4] {'context'}, use_global_device_ids=true, to_apply=%add | all-reduce | flops 8 | bytes 32
  29.2 0.1 compare_and_fusion
  29.3 0.0 copy-done
  29.3 1.4 convolution_bitcast_fusion
  30.7 32.3 %all-gather.6.cloned.1.call-done = bf16[64,128,128]{2,1,0:T(8,128)(2,1)} async-done(((bf16[8,128,128]{2,1,0:T(8,128)(2,1)}), bf16[64,128,128]{2,1,0:T(8,128)(2,1)}) %all-gather.6.cloned.1.call-update) | async-done | bytes 2097168 | tf_op jit(solution)/shard_map/all_gather | solution.py:15
  63.0 0.0 copy-start.3
  63.1 7.2 %while.12 = (s32[]{:T(128)}, f32[8,128,128]{2,1,0:T(8,128)S(1)}, s32[]{:T(128)}, bf16[8]{0:T(256)(128)(2,1)S(1)}, bf16[8,8,128,128]{3,2,1,0:T(8,128)(2,1)}, /*index=5*/s32[]{:T(128)}, s32[]{:T(128)}, s32[]{:T(128)}, f32[1]{0:T(128)}) while((s32[]{:T(128)}, f32[8,128,128]{2,1,0:T(8,128)S(1)}, s32[]{:T(128)}, bf16[8]{0:T(256)(128)(2,1)S(1)}, ...), condition=%wide.region_4.5_spmd, body=%wide.region_3.4_spmd.sunk | while | flops 393222 | bytes 1310867 | solution.py:29
  63.1 0.6 dynamic_slice.14
  64.3 1.1 add_select_fusion.2
  65.5 0.6 dynamic_slice.14
  66.7 1.1 add_select_fusion.2
  67.9 0.6 dynamic_slice.14
  69.1 1.1 add_select_fusion.2
  70.2 0.3 multiply_reduce_fusion
  70.6 0.0 copy-done.3
  70.6 0.2 multiply_convert_fusion
  70.8 0.0 copy-start.1
  70.8 7.6 %convolution_convert_fusion = bf16[128,6144]{1,0:T(8,128)(2,1)} fusion(bf16[128,1024]{0,1:T(8,128)(2,1)S(1)} %bitcast.69, bf16[1024,6144]{1,0:T(8,128)(2,1)} %param.15), kind=kOutput, calls=%fused_computation.1 | convolution fusion | flops 1611399168 | bytes 14417920 | tf_op jit(solution)/shard_map/dot_general | solution.py:91
  78.5 0.0 reduce-scatter.2.cloned.1.call-update
  78.5 0.0 all-gather.4.cloned.1.call-start
  78.5 0.0 copy-done.1
  78.6 10.7 %all_to_all.32 = bf16[4,32,1536]{2,1,0:T(8,128)(2,1)S(1)} all-to-all(bf16[4,32,1536]{2,1,0:T(8,128)(2,1)S(1)} %bitcast.73), channel_id=1, replica_groups=mesh['context'=8,'tensor'=4] {'tensor'}, dimensions={0} | all-to-all | bytes 786432 | tf_op jit(solution)/shard_map/all_to_all | solution.py:96
  89.2 0.0 copy-start.2
  89.2 0.1 convert_bitcast_fusion
  89.3 0.1 copy.51
  89.4 27.2 %reduce-scatter.2.cloned.1.call-done = bf16[32,6144]{1,0:T(8,128)(2,1)} async-done(((bf16[128,6144]{1,0:T(8,128)(2,1)}), bf16[32,6144]{1,0:T(8,128)(2,1)}) %reduce-scatter.2.cloned.1.call-update) | async-done | bytes 393232 | tf_op jit(solution)/shard_map/reduce_scatter | solution.py:90
  116.6 1.2 fusion.3
  117.8 0.0 copy-done.2
  117.8 0.9 fusion.5
  118.7 0.0 all-gather.4.cloned.1.call-update
  118.8 9.6 %all_to_all.33 = bf16[32,4,1536]{2,0,1:T(8,128)(2,1)S(1)} all-to-all(bf16[32,4,1536]{2,0,1:T(8,128)(2,1)S(1)} %bitcast.68), channel_id=1, replica_groups=mesh['context'=8,'tensor'=4] {'tensor'}, dimensions={1} | all-to-all | bytes 786432 | tf_op jit(solution)/shard_map/all_to_all | solution.py:100
  128.4 10.7 %all-gather.4.cloned.1.call-done = bf16[128,6144]{1,0:T(8,128)(2,1)} async-done(((bf16[32,6144]{1,0:T(8,128)(2,1)}), bf16[128,6144]{1,0:T(8,128)(2,1)}) %all-gather.4.cloned.1.call-update) | async-done | bytes 1572880 | tf_op jit(solution)/shard_map/all_gather | solution.py:99
  139.1 0.7 copy.82
  139.8 2.7 %copy.83 = bf16[128,6144]{1,0:T(8,128)(2,1)} copy(bf16[128,6144]{1,0:T(8,128)(2,1)} %all-gather.4.cloned.1.call-done) | data formatting | bytes 3145728
  (8 shorter events, 0.1 us)
Async XLA Ops:
  7.2 22.2 %copy-start = (bf16[128,1024]{1,0:T(8,128)(2,1)S(1)}, bf16[128,1024]{1,0:T(8,128)(2,1)}, u32[]{:S(2)}) copy-start(bf16[128,1024]{1,0:T(8,128)(2,1)} %param.10) | copy-start | bytes 786436
  7.2 55.8 %all-gather.6.cloned.1.call-start = ((), (), s32[]{:S(2)}) async-start(), calls=%async_computation.5 | async-start | bytes 2359296 | tf_op jit(solution)/shard_map/all_gather | solution.py:15
  14.4 102.1 %reduce-scatter.2.cloned.1.call-start = ((), (), s32[]{:S(2)}) async-start(), calls=%async_computation.3 | async-start | bytes 1966080 | tf_op jit(solution)/shard_map/reduce_scatter | solution.py:90
  63.0 7.6 %copy-start.3 = (f32[1024]{0:T(1024)S(1)}, f32[1024]{0:T(1024)}, u32[]{:S(2)}) copy-start(f32[1024]{0:T(1024)} %param.14) | copy-start | bytes 12292
  70.8 7.7 %copy-start.1 = (bf16[128,1536]{1,0:T(8,128)(2,1)S(1)}, bf16[128,1536]{1,0:T(8,128)(2,1)}, u32[]{:S(2)}) copy-start(bf16[128,1536]{1,0:T(8,128)(2,1)} %param.16) | copy-start | bytes 1179652
  78.5 60.6 %all-gather.4.cloned.1.call-start = ((), (), s32[]{:S(2)}) async-start(), calls=%async_computation.4 | async-start | bytes 1966080 | tf_op jit(solution)/shard_map/all_gather | solution.py:99
  89.2 28.6 %copy-start.2 = (f32[6144]{0:T(1024)S(1)}, f32[6144]{0:T(1024)}, u32[]{:S(2)}) copy-start(f32[6144]{0:T(1024)} %param.17) | copy-start | bytes 73732
Sparse Core Ops, SparseCore 0:
  14.5 48.4 all-gather.5
  78.6 37.8 reduce-scatter.1
  118.9 20.1 all-gather.3
where the time goes:
time: 151 us; the launch traced here: 149 us
  waiting for transfers between devices  70.2 us (46%)
  blocking collectives  32.4 us (21%)
  between operations  15.2 us (10%)
  matrix products  11.3 us (7%)
  local copies, waits for them, and re-layouts  9.78 us (6%)
  other arithmetic  8.04 us (5%)
  loops' own time  2.06 us (1%)
    all_gather x1, waiting for transfers between devices, entering(): lax.all_gather(a.astype(kind), axis)  32.3 us
    reduce_scatter x1, waiting for transfers between devices, local(): lax.psum_scatter(jnp.dot(head_out, output_weight, preferred_element_type=...  27.2 us
    unnamed x1, blocking collectives  12.1 us
    all_gather x1, waiting for transfers between devices, local(): normed = lax.all_gather(normed_part, 'tensor', axis=0, tiled=True)  10.7 us
    all_to_all x1, blocking collectives, local(): lax.all_to_all(residual, 'tensor', split_axis=0, concat_axis=1, tiled=True)  10.7 us
    all_to_all x1, blocking collectives, local(): lax.all_to_all(hidden_rows, 'tensor', split_axis=1, concat_axis=0, tiled=...  9.62 us
    dot_general x1, matrix products, local(): jnp.dot(head_out, output_weight, preferred_element_type=jnp.float32)  7.65 us
    unnamed x13, local copies, waits for them, and re-layouts  5.46 us
  transfers between devices with their start and end apart: 3, of which 3 were waited for; matrix products, arithmetic and copies ran while one was open for 2% of the time, Pallas kernels for 0%

commit v1 on v0

v1 whole, which is shorter than its diff:
```python
import functools

import jax
import jax.numpy as jnp
from jax import lax
from jax.experimental import pallas as pl
from jax.experimental.pallas import tpu as pltpu
from jax.sharding import PartitionSpec as P

HEAD = 128
EPSILON = 1e-06
DOC_SHARE = 4
SUBS = 3
F32 = jnp.float32
BF16 = jnp.bfloat16


def kernel(
    n_context, n_tensor, reach, doc_count,
    lens, gain, final_gain, q, k, v, res, w_hbm,
    ns_out, nm_out,
    wbuf, st_send, st_recv, st_acc, inner, head_out,
    p_send, p_recv, keep, c_send, c_recv, hid,
    w_sem, st_ss, st_rs, p_ss, p_rs, c_ss, c_rs, g_ss, g_rs, h_ss, h_rs, r_ss, r_rs,
):
    c = lax.axis_index("context")
    t = lax.axis_index("tensor")
    rows = n_tensor // 2
    y, core = t // 2, t % 2
    mate = y * 2 + (1 - core)
    tok, width = q.shape
    heads = width // HEAD
    sub = p_send.shape[-1]
    part = sub * SUBS

    def there(dy):
        return lax.rem(y + dy, rows) if rows > 1 else y

    def back(dy):
        return lax.rem(y - dy + rows, rows) if rows > 1 else y

    def remote(src, dst, ss, rs, context, tensor):
        return pltpu.make_async_remote_copy(
            src_ref=src, dst_ref=dst, send_sem=ss, recv_sem=rs,
            device_id={"context": context, "tensor": tensor},
            device_id_type=pl.DeviceIdType.MESH,
        )

    order = [(dy, s) for s in range(SUBS) for dy in range(1, rows)] + [(0, s) for s in range(SUBS)]
    w_copies = []
    for g, (dy, s) in enumerate(order):
        for mine in range(2):
            owner = there(dy) * 2 + (core if mine else 1 - core)
            col = pl.multiple_of(owner * part + s * sub, 128)
            w_copies.append(
                pltpu.make_async_copy(
                    w_hbm.at[:, pl.ds(col, sub)], wbuf.at[2 * g + mine], w_sem.at[2 * g + mine]
                )
            )

    barrier = pltpu.get_barrier_semaphore()

    def greet(context, tensor):
        pl.semaphore_signal(
            barrier, inc=1, device_id={"context": context, "tensor": tensor},
            device_id_type=pl.DeviceIdType.MESH,
        )

    for j in range(1, reach + 1):
        @pl.when(c >= j)
        def _():
            greet(c - j, t)

        @pl.when(c + j < n_context)
        def _():
            greet(c + j, t)

    greet(c, mate)
    for dy in range(1, rows):
        greet(c, there(dy) * 2 + core)

    for copy in w_copies:
        copy.start()

    starts, total = [], jnp.int32(0)
    for i in range(doc_count):
        starts.append(total)
        total = total + lens[i]

    def doc_of(pos):
        count = jnp.zeros_like(pos) - 1
        for start in starts:
            count = count + (pos >= start).astype(jnp.int32)
        return count

    first = c * tok
    row = lax.broadcasted_iota(jnp.int32, (tok, tok), 0)
    column = lax.broadcasted_iota(jnp.int32, (tok, tok), 1)
    doc_row, doc_col = doc_of(row + first), doc_of(column + first)
    row_h = lax.broadcasted_iota(jnp.int32, (tok, HEAD), 0) + first
    doc_h = doc_of(row_h)
    prev_doc, last_doc = doc_of(first - 1), doc_of(first + tok - 1)
    last_mask = doc_h == last_doc
    carry_mask = doc_h == prev_doc
    causal = (column <= row) & (doc_row == doc_col)

    for h in range(heads):
        cols = slice(h * HEAD, (h + 1) * HEAD)
        masked = jnp.where(last_mask, k[:, cols].astype(F32), 0.0).astype(BF16)
        st_send[:, cols] = lax.dot_general(
            masked, v[:, cols], (((0,), (0,)), ((), ())), preferred_element_type=F32
        ).astype(BF16)

    pl.semaphore_wait(
        barrier, jnp.minimum(c, reach) + jnp.minimum(n_context - 1 - c, reach) + rows
    )

    def state_copy(j, target):
        return remote(st_send, st_recv.at[j - 1], st_ss.at[j - 1], st_rs.at[j - 1], target, t)

    for j in range(1, reach + 1):
        @pl.when(c + j < n_context)
        def _():
            state_copy(j, c + j).start()

    for h in range(heads):
        cols = slice(h * HEAD, (h + 1) * HEAD)
        scores = lax.dot_general(
            q[:, cols], k[:, cols], (((1,), (1,)), ((), ())), preferred_element_type=F32
        )
        weights = jnp.where(causal, scores, 0.0).astype(BF16)
        inner[:, cols] = jnp.dot(weights, v[:, cols], preferred_element_type=F32)

    st_acc[...] = jnp.zeros_like(st_acc)
    for j in range(1, reach + 1):
        same = (doc_of(first - (j - 1) * tok - 1) == prev_doc).astype(F32)

        @pl.when(c >= j)
        def _():
            state_copy(j, c - j).wait_recv()
            st_acc[...] += st_recv[j - 1].astype(F32) * same

    for h in range(heads):
        cols = slice(h * HEAD, (h + 1) * HEAD)
        cross = jnp.dot(q[:, cols], st_acc[:, cols].astype(BF16), preferred_element_type=F32)
        attention = inner[:, cols] + jnp.where(carry_mask, cross, 0.0)
        squares = jnp.mean(attention * attention, axis=-1, keepdims=True)
        head_out[:, cols] = (attention * lax.rsqrt(squares + EPSILON) * gain[:, cols]).astype(BF16)

    def slot(dy, s):
        return dy * SUBS + s

    def mate_copy(dy, s):
        i = slot(dy, s)
        return remote(p_send.at[i], p_recv.at[i], p_ss.at[i], p_rs.at[i], c, mate)

    def cross_copy(dy, s):
        i = slot(dy - 1, s)
        return remote(
            c_send.at[i], c_recv.at[i], c_ss.at[i], c_rs.at[i], c, there(dy) * 2 + core
        )

    def pass_on(dy, s):
        mate_copy(dy, s).wait_recv()
        c_send[slot(dy - 1, s)] = (
            keep[slot(dy, s)] + p_recv[slot(dy, s)].astype(F32)
        ).astype(BF16)
        cross_copy(dy, s).start()

    waiting = None
    for g, (dy, s) in enumerate(order):
        w_copies[2 * g].wait()
        p_send[slot(dy, s)] = jnp.dot(
            head_out[...], wbuf[2 * g], preferred_element_type=F32
        ).astype(BF16)
        mate_copy(dy, s).start()
        w_copies[2 * g + 1].wait()
        keep[slot(dy, s)] = jnp.dot(head_out[...], wbuf[2 * g + 1], preferred_element_type=F32)
        if waiting is not None:
            pass_on(*waiting)
        waiting = (dy, s) if dy else None

    def own_copy(s):
        i = t * SUBS + s
        return remote(hid.at[i], hid.at[i], h_ss.at[s], h_rs.at[s], c, mate)

    def far_copy(dy, s):
        i = slot(dy - 1, s)
        place = t * SUBS + s
        return remote(
            hid.at[place], hid.at[place], g_ss.at[i], g_rs.at[i], c, there(dy) * 2 + core
        )

    def relay_copy(dy, s):
        i = slot(dy - 1, s)
        place = (back(dy) * 2 + core) * SUBS + s
        return remote(hid.at[place], hid.at[place], r_ss.at[i], r_rs.at[i], c, mate)

    def squared(piece):
        rest = 0.0
        x = piece.astype(F32)
        for b in range(0, sub, 128):
            rest = rest + x[:, b : b + 128] * x[:, b : b + 128]
        return rest

    sums = jnp.zeros((tok, 128), F32)
    for s in range(SUBS):
        mate_copy(0, s).wait_recv()
        added = keep[slot(0, s)] + p_recv[slot(0, s)].astype(F32)
        for dy in range(1, rows):
            cross_copy(dy, s).wait_recv()
            added = added + c_recv[slot(dy - 1, s)].astype(F32)
        cols = slice(s * sub, (s + 1) * sub)
        new = (added + res[:, cols].astype(F32)).astype(BF16)
        hid[t * SUBS + s] = new
        for dy in range(1, rows):
            far_copy(dy, s).start()
        own_copy(s).start()
        ns_out[:, cols] = new
        sums = sums + squared(new)

    for s in range(SUBS):
        own_copy(s).wait_recv()
        sums = sums + squared(hid[mate * SUBS + s])
    for s in range(SUBS):
        for dy in range(1, rows):
            far_copy(dy, s).wait_recv()
            relay_copy(dy, s).start()
            sums = sums + squared(hid[(back(dy) * 2 + core) * SUBS + s])
    for s in range(SUBS):
        for dy in range(1, rows):
            relay_copy(dy, s).wait_recv()
            sums = sums + squared(hid[(back(dy) * 2 + 1 - core) * SUBS + s])

    mean = jnp.sum(sums, axis=-1, keepdims=True) * (1.0 / (part * n_tensor))
    scale = lax.rsqrt(mean + EPSILON)
    for i in range(n_tensor * SUBS):
        cols = slice(i * sub, (i + 1) * sub)
        nm_out[:, cols] = (hid[i].astype(F32) * scale * final_gain[:, cols]).astype(BF16)

    for j in range(1, reach + 1):
        @pl.when(c + j < n_context)
        def _():
            state_copy(j, c + j).wait_send()
    for s in range(SUBS):
        own_copy(s).wait_send()
        mate_copy(0, s).wait_send()
        for dy in range(1, rows):
            mate_copy(dy, s).wait_send()
            cross_copy(dy, s).wait_send()
            far_copy(dy, s).wait_send()
            relay_copy(dy, s).wait_send()


def solution(mesh):
    n_context, n_tensor = mesh.shape["context"], mesh.shape["tensor"]

    def local(q, k, v, lens, gain, weight, res, final_gain):
        tok, width = q.shape
        model = weight.shape[1]
        part = model // n_tensor
        sub = part // SUBS
        rows = n_tensor // 2
        longest = tok * n_context // DOC_SHARE
        reach = min(n_context - 1, max(1, -(-longest // tok)))
        pieces = rows * SUBS
        far = max(1, (rows - 1) * SUBS)
        dma = pltpu.SemaphoreType.DMA
        vmem = pl.BlockSpec(memory_space=pltpu.VMEM)
        return pl.pallas_call(
            functools.partial(kernel, n_context, n_tensor, reach, lens.shape[0]),
            name="layer",
            out_shape=(
                jax.ShapeDtypeStruct((tok, part), BF16),
                jax.ShapeDtypeStruct((tok, model), BF16),
            ),
            in_specs=[pl.BlockSpec(memory_space=pltpu.SMEM)] + [vmem] * 6
            + [pl.BlockSpec(memory_space=pl.ANY)],
            out_specs=(vmem, vmem),
            scratch_shapes=[
                pltpu.VMEM((2 * pieces, width, sub), BF16),
                pltpu.VMEM((HEAD, width), BF16),
                pltpu.VMEM((reach, HEAD, width), BF16),
                pltpu.VMEM((HEAD, width), F32),
                pltpu.VMEM((tok, width), F32),
                pltpu.VMEM((tok, width), BF16),
                pltpu.VMEM((pieces, tok, sub), BF16),
                pltpu.VMEM((pieces, tok, sub), BF16),
                pltpu.VMEM((pieces, tok, sub), F32),
                pltpu.VMEM((far, tok, sub), BF16),
                pltpu.VMEM((far, tok, sub), BF16),
                pltpu.VMEM((n_tensor * SUBS, tok, sub), BF16),
                dma((2 * pieces,)),
                dma((reach,)), dma((reach,)),
                dma((pieces,)), dma((pieces,)),
                dma((far,)), dma((far,)),
                dma((far,)), dma((far,)),
                dma((SUBS,)), dma((SUBS,)),
                dma((far,)), dma((far,)),
            ],
            compiler_params=pltpu.CompilerParams(
                collective_id=0, has_side_effects=True, vmem_limit_bytes=60 * 1024 * 1024
            ),
        )(lens, gain.reshape(1, -1), final_gain.reshape(1, -1), q, k, v, res, weight)

    return jax.shard_map(
        local,
        mesh=mesh,
        in_specs=(
            P("context", "tensor"), P("context", "tensor"), P("context", "tensor"), P(),
            P("tensor"), P("tensor", None), P("context", "tensor"), P(),
        ),
        out_specs=(P("context", "tensor"), P("context", None)),
        check_vma=False,
    )
```

time: 151 us -> 45.5 us (0.30); the launches traced: 149 us -> 45.3 us
  waiting for transfers between devices: 70.2 us -> 0 us
  Pallas kernels: 0 us -> 40.2 us
  blocking collectives: 32.4 us -> 0 us
  between operations: 15.2 us -> 0.64 us
  matrix products: 11.3 us -> 0 us
  other arithmetic: 8.04 us -> 0 us
  local copies, waits for them, and re-layouts: 9.78 us -> 4.46 us
  loops' own time: 2.06 us -> 0 us
    all_gather x2 -> x0, waiting for transfers between devices: 43 us -> none  [the longest x1 32.3 us: entering(): lax.all_gather(a.astype(kind), axis)]
    pallas_call x0 -> x1, Pallas kernels: none -> 40.2 us  [local(): pl.pallas_call(functools.partial(kernel, n_context, n_tensor, reach, lens...]
    reduce_scatter x1 -> x0, waiting for transfers between devices: 27.2 us -> none  [local(): lax.psum_scatter(jnp.dot(head_out, output_weight, preferred_element_type=...]
    all_to_all x2 -> x0, blocking collectives: 20.3 us -> none  [the longest x1 10.7 us: local(): lax.all_to_all(residual, 'tensor', split_axis=0, concat_axis=1, tiled=True)]
    unnamed x1 -> x0, blocking collectives: 12.1 us -> none
    dot_general x4 -> x0, matrix products: 11.3 us -> none  [the longest x1 7.65 us: local(): jnp.dot(head_out, output_weight, preferred_element_type=jnp.float32)]
    select_n x3 -> x0, other arithmetic: 3.36 us -> none  [combine_states(): jnp.where(later[0] > 0.5, later[1], earlier[1] + later[1])]
    reduce_sum x3 -> x0, other arithmetic: 2.6 us -> none  [the longest x2 1.38 us: doc_index(): jnp.sum((positions[:, None] >= starts[None, :]).astype(jnp.int32), axis=1)]
  transfers between devices with their start and end apart: 3 -> 0, of which waited for: 3 -> 0; matrix products, arithmetic and copies ran while one was open for 2% -> 0% of each run, Pallas kernels for 0% -> 0%
where the time goes in v1:
time: 45.5 us; the launch traced here: 45.3 us
  Pallas kernels  40.2 us (88%)
  local copies, waits for them, and re-layouts  4.46 us (10%)
  between operations  0.64 us (1%)
    pallas_call x1, Pallas kernels, local(): pl.pallas_call(functools.partial(kernel, n_context, n_tensor, reach, lens...  40.2 us
    unnamed x2, local copies, waits for them, and re-layouts  4.46 us

profile of v1, /device:TPU:11, one launch (start us, length us, event | category | flops | bytes accessed | tf_op | source)
XLA Modules:
  0.0 45.3 jit_solution(5350711185021639217)
XLA Ops:
  0.6 40.2 %layer.1 = (bf16[128,1536]{1,0:T(8,128)(2,1)}, bf16[128,6144]{1,0:T(8,128)(2,1)}) custom-call(s32[16]{0:T(128)} %lens.1, f32[1,1024]{1,0:T(1,128)} %bitcast.3, f32[1,6144]{1,0:T(1,128)} %bitcast.2, bf16[128,1024]{1,0:T(8,128)(2,1)} %q.1, bf16[128,1024]{1,0:T(8,128)(2,1)} %k.1, bf16[128,1024]{1,0:T(8,128)(2,1)} %v.1, bf16[128,1536]{1,0:T(8,128)(2,1)} %res.1, ...), custom_call_target="tpu_custom_call" | custom-call | tf_op jit(solution)/shard_map/layer/pallas_call | solution.py:270
  40.8 1.8 %copy.12 = bf16[128,1536]{1,0:T(8,128)(2,1)} copy(bf16[128,1536]{1,0:T(8,128)(2,1)} %get-tuple-element.4) | data formatting | bytes 786432
  42.6 2.7 %copy.13 = bf16[128,6144]{1,0:T(8,128)(2,1)} copy(bf16[128,6144]{1,0:T(8,128)(2,1)} %get-tuple-element.5) | data formatting | bytes 3145728

commit v2 on v1

--- a/solution.py
+++ b/solution.py
@@ -16,12 +16,12 @@
 
 
 def kernel(
-    n_context, n_tensor, reach, doc_count,
-    lens, gain, final_gain, q, k, v, res, w_hbm,
-    ns_out, nm_out,
+    n_context, n_tensor, reach, cuts, relayed, doc_count,
+    lens, gain, q, k, v, res, w_hbm,
+    ns_out, hid_out, scale_out,
     wbuf, st_send, st_recv, st_acc, inner, head_out,
     p_send, p_recv, keep, c_send, c_recv, hid,
-    w_sem, st_ss, st_rs, p_ss, p_rs, c_ss, c_rs, g_ss, g_rs, h_ss, h_rs, r_ss, r_rs,
+    w_sem, st_ss, st_rs, p_ss, p_rs, c_ss, c_rs, g_ss, g_rs, h_ss, h_rs, r_ss, r_rs, z_ss, o_sem, n_sem,
 ):
     c = lax.axis_index("context")
     t = lax.axis_index("tensor")
@@ -104,24 +104,36 @@
     carry_mask = doc_h == prev_doc
     causal = (column <= row) & (doc_row == doc_col)
 
-    for h in range(heads):
-        cols = slice(h * HEAD, (h + 1) * HEAD)
-        masked = jnp.where(last_mask, k[:, cols].astype(F32), 0.0).astype(BF16)
-        st_send[:, cols] = lax.dot_general(
-            masked, v[:, cols], (((0,), (0,)), ((), ())), preferred_element_type=F32
-        ).astype(BF16)
-
-    pl.semaphore_wait(
-        barrier, jnp.minimum(c, reach) + jnp.minimum(n_context - 1 - c, reach) + rows
-    )
-
-    def state_copy(j, target):
-        return remote(st_send, st_recv.at[j - 1], st_ss.at[j - 1], st_rs.at[j - 1], target, t)
-
-    for j in range(1, reach + 1):
-        @pl.when(c + j < n_context)
-        def _():
-            state_copy(j, c + j).start()
+    each = width // cuts
+
+    def state_copy(j, m, target):
+        i = (j - 1) * cuts + m
+        return remote(st_send.at[m], st_recv.at[i], st_ss.at[i], st_rs.at[i], target, t)
+
+    def relay_state(m):
+        return remote(st_recv.at[cuts + m], st_recv.at[m], z_ss.at[m], st_rs.at[m], c - 1, t)
+
+    def sends(j):
+        go = c + j < n_context
+        return go & (lax.rem(c, 2) == 0) if relayed and j == 1 else go
+
+    relays = (lax.rem(c, 2) == 1) & (c >= 3)
+
+    for m in range(cuts):
+        for h in range(each // HEAD):
+            cols = slice(m * each + h * HEAD, m * each + (h + 1) * HEAD)
+            masked = jnp.where(last_mask, k[:, cols].astype(F32), 0.0).astype(BF16)
+            st_send[m, :, h * HEAD : (h + 1) * HEAD] = lax.dot_general(
+                masked, v[:, cols], (((0,), (0,)), ((), ())), preferred_element_type=F32
+            ).astype(BF16)
+        if m == 0:
+            pl.semaphore_wait(
+                barrier, jnp.minimum(c, reach) + jnp.minimum(n_context - 1 - c, reach) + rows
+            )
+        for j in range(reach, 0, -1):
+            @pl.when(sends(j))
+            def _():
+                state_copy(j, m, c + j).start()
 
     for h in range(heads):
         cols = slice(h * HEAD, (h + 1) * HEAD)
@@ -132,20 +144,28 @@
         inner[:, cols] = jnp.dot(weights, v[:, cols], preferred_element_type=F32)
 
     st_acc[...] = jnp.zeros_like(st_acc)
-    for j in range(1, reach + 1):
-        same = (doc_of(first - (j - 1) * tok - 1) == prev_doc).astype(F32)
-
-        @pl.when(c >= j)
-        def _():
-            state_copy(j, c - j).wait_recv()
-            st_acc[...] += st_recv[j - 1].astype(F32) * same
-
-    for h in range(heads):
-        cols = slice(h * HEAD, (h + 1) * HEAD)
-        cross = jnp.dot(q[:, cols], st_acc[:, cols].astype(BF16), preferred_element_type=F32)
-        attention = inner[:, cols] + jnp.where(carry_mask, cross, 0.0)
-        squares = jnp.mean(attention * attention, axis=-1, keepdims=True)
-        head_out[:, cols] = (attention * lax.rsqrt(squares + EPSILON) * gain[:, cols]).astype(BF16)
+    for m in range(cuts):
+        piece = slice(m * each, (m + 1) * each)
+        for j in range(reach, 0, -1):
+            same = (doc_of(first - (j - 1) * tok - 1) == prev_doc).astype(F32)
+
+            @pl.when(c >= j)
+            def _():
+                state_copy(j, m, c - j).wait_recv()
+                if relayed and j == 2:
+                    @pl.when(relays)
+                    def _():
+                        relay_state(m).start()
+                st_acc[:, piece] += st_recv[(j - 1) * cuts + m].astype(F32) * same
+
+        for h in range(m * each // HEAD, (m + 1) * each // HEAD):
+            cols = slice(h * HEAD, (h + 1) * HEAD)
+            cross = jnp.dot(q[:, cols], st_acc[:, cols].astype(BF16), preferred_element_type=F32)
+            attention = inner[:, cols] + jnp.where(carry_mask, cross, 0.0)
+            squares = jnp.mean(attention * attention, axis=-1, keepdims=True)
+            head_out[:, cols] = (
+                attention * lax.rsqrt(squares + EPSILON) * gain[:, cols]
+            ).astype(BF16)
 
     def slot(dy, s):
         return dy * SUBS + s
@@ -203,6 +223,14 @@
             rest = rest + x[:, b : b + 128] * x[:, b : b + 128]
         return rest
 
+    def out_copy(i):
+        return pltpu.make_async_copy(hid.at[i], hid_out.at[i], o_sem.at[i])
+
+    def stream_copy(s):
+        return pltpu.make_async_copy(
+            hid.at[t * SUBS + s], ns_out.at[:, pl.ds(s * sub, sub)], n_sem.at[s]
+        )
+
     sums = jnp.zeros((tok, 128), F32)
     for s in range(SUBS):
         mate_copy(0, s).wait_recv()
@@ -216,32 +244,42 @@
         for dy in range(1, rows):
             far_copy(dy, s).start()
         own_copy(s).start()
-        ns_out[:, cols] = new
+        stream_copy(s).start()
+        out_copy(t * SUBS + s).start()
         sums = sums + squared(new)
 
     for s in range(SUBS):
         own_copy(s).wait_recv()
+        out_copy(mate * SUBS + s).start()
         sums = sums + squared(hid[mate * SUBS + s])
     for s in range(SUBS):
         for dy in range(1, rows):
             far_copy(dy, s).wait_recv()
             relay_copy(dy, s).start()
+            out_copy((back(dy) * 2 + core) * SUBS + s).start()
             sums = sums + squared(hid[(back(dy) * 2 + core) * SUBS + s])
     for s in range(SUBS):
         for dy in range(1, rows):
             relay_copy(dy, s).wait_recv()
+            out_copy((back(dy) * 2 + 1 - core) * SUBS + s).start()
             sums = sums + squared(hid[(back(dy) * 2 + 1 - core) * SUBS + s])
 
     mean = jnp.sum(sums, axis=-1, keepdims=True) * (1.0 / (part * n_tensor))
-    scale = lax.rsqrt(mean + EPSILON)
+    scale_out[...] = jnp.broadcast_to(lax.rsqrt(mean + EPSILON), (tok, 128))
+
+    for m in range(cuts):
+        for j in range(1, reach + 1):
+            @pl.when(sends(j))
+            def _():
+                state_copy(j, m, c + j).wait_send()
+        if relayed:
+            @pl.when(relays)
+            def _():
+                relay_state(m).wait_send()
     for i in range(n_tensor * SUBS):
-        cols = slice(i * sub, (i + 1) * sub)
-        nm_out[:, cols] = (hid[i].astype(F32) * scale * final_gain[:, cols]).astype(BF16)
-
-    for j in range(1, reach + 1):
-        @pl.when(c + j < n_context)
-        def _():
-            state_copy(j, c + j).wait_send()
+        out_copy(i).wait()
+    for s in range(SUBS):
+        stream_copy(s).wait()
     for s in range(SUBS):
         own_copy(s).wait_send()
         mate_copy(0, s).wait_send()
@@ -250,6 +288,21 @@
             cross_copy(dy, s).wait_send()
             far_copy(dy, s).wait_send()
             relay_copy(dy, s).wait_send()
+
+
+def finish(ns, hid, scale, final_gain, ns_out, nm_out):
+    sub = hid.shape[-1]
+
+    @pl.when(pl.program_id(0) == 0)
+    def _():
+        ns_out[...] = ns[...]
+
+    for s in range(SUBS):
+        for b in range(0, sub, 128):
+            cols = slice(s * sub + b, s * sub + b + 128)
+            nm_out[:, cols] = (
+                hid[s, :, b : b + 128].astype(F32) * scale[...] * final_gain[:, cols]
+            ).astype(BF16)
 
 
 def solution(mesh):
@@ -265,22 +318,28 @@
         reach = min(n_context - 1, max(1, -(-longest // tok)))
         pieces = rows * SUBS
         far = max(1, (rows - 1) * SUBS)
+        relayed = reach == 2 and n_context % 2 == 0
+        cuts = 4 if relayed else 1
+        count = n_tensor * SUBS
         dma = pltpu.SemaphoreType.DMA
         vmem = pl.BlockSpec(memory_space=pltpu.VMEM)
-        return pl.pallas_call(
-            functools.partial(kernel, n_context, n_tensor, reach, lens.shape[0]),
+        ns, hid, scale = pl.pallas_call(
+            functools.partial(kernel, n_context, n_tensor, reach, cuts, relayed, lens.shape[0]),
             name="layer",
             out_shape=(
                 jax.ShapeDtypeStruct((tok, part), BF16),
-                jax.ShapeDtypeStruct((tok, model), BF16),
-            ),
-            in_specs=[pl.BlockSpec(memory_space=pltpu.SMEM)] + [vmem] * 6
+                jax.ShapeDtypeStruct((count, tok, sub), BF16),
+                jax.ShapeDtypeStruct((tok, 128), F32),
+            ),
+            in_specs=[pl.BlockSpec(memory_space=pltpu.SMEM)] + [vmem] * 5
             + [pl.BlockSpec(memory_space=pl.ANY)],
-            out_specs=(vmem, vmem),
+            out_specs=(
+                pl.BlockSpec(memory_space=pl.ANY), pl.BlockSpec(memory_space=pl.ANY), vmem
+            ),
             scratch_shapes=[
                 pltpu.VMEM((2 * pieces, width, sub), BF16),
-                pltpu.VMEM((HEAD, width), BF16),
-                pltpu.VMEM((reach, HEAD, width), BF16),
+                pltpu.VMEM((cuts, HEAD, width // cuts), BF16),
+                pltpu.VMEM((reach * cuts, HEAD, width // cuts), BF16),
                 pltpu.VMEM((HEAD, width), F32),
                 pltpu.VMEM((tok, width), F32),
                 pltpu.VMEM((tok, width), BF16),
@@ -291,17 +350,37 @@
                 pltpu.VMEM((far, tok, sub), BF16),
                 pltpu.VMEM((n_tensor * SUBS, tok, sub), BF16),
                 dma((2 * pieces,)),
-                dma((reach,)), dma((reach,)),
+                dma((reach * cuts,)), dma((reach * cuts,)),
                 dma((pieces,)), dma((pieces,)),
                 dma((far,)), dma((far,)),
                 dma((far,)), dma((far,)),
                 dma((SUBS,)), dma((SUBS,)),
                 dma((far,)), dma((far,)),
+                dma((cuts,)), dma((count,)), dma((SUBS,)),
             ],
             compiler_params=pltpu.CompilerParams(
                 collective_id=0, has_side_effects=True, vmem_limit_bytes=60 * 1024 * 1024
             ),
-        )(lens, gain.reshape(1, -1), final_gain.reshape(1, -1), q, k, v, res, weight)
+        )(lens, gain.reshape(1, -1), q, k, v, res, weight)
+        return pl.pallas_call(
+            finish,
+            name="finish",
+            grid=(n_tensor,),
+            out_shape=(
+                jax.ShapeDtypeStruct((tok, part), BF16),
+                jax.ShapeDtypeStruct((tok, model), BF16),
+            ),
+            in_specs=[
+                pl.BlockSpec((tok, part), lambda i: (0, 0)),
+                pl.BlockSpec((SUBS, tok, sub), lambda i: (i, 0, 0)),
+                pl.BlockSpec((tok, 128), lambda i: (0, 0)),
+                pl.BlockSpec((1, part), lambda i: (0, i)),
+            ],
+            out_specs=(
+                pl.BlockSpec((tok, part), lambda i: (0, 0)),
+                pl.BlockSpec((tok, part), lambda i: (0, i)),
+            ),
+        )(ns, hid, scale, final_gain.reshape(1, -1))
 
     return jax.shard_map(
         local,

time: 45.5 us -> 43 us (0.945)
  the two profiles are of different devices: /device:TPU:11 before, /device:TPU:17 now
where the time goes in v2:
time: 43 us; the launch traced here: 42.8 us
  Pallas kernels  42.2 us (98%)
  between operations  0.64 us (1%)
    pallas_call x1, Pallas kernels, local(): pl.pallas_call(functools.partial(kernel, n_context, n_tensor, reach, cuts...  38.3 us
    pallas_call x1, Pallas kernels, local(): pl.pallas_call(finish, name='finish', grid=(n_tensor,), out_shape=(jax.Sh...  3.94 us

profile of v2, /device:TPU:17, one launch (start us, length us, event | category | flops | bytes accessed | tf_op | source)
XLA Modules:
  0.0 42.8 jit_solution(6110246336515611791)
XLA Ops:
  0.6 38.3 %layer.1 = (bf16[128,1536]{1,0:T(8,128)(2,1)}, bf16[12,128,512]{2,1,0:T(8,128)(2,1)}, f32[128,128]{1,0:T(8,128)}) custom-call(s32[16]{0:T(128)} %lens.1, f32[1,1024]{1,0:T(1,128)} %bitcast.3, bf16[128,1024]{1,0:T(8,128)(2,1)} %q.1, bf16[128,1024]{1,0:T(8,128)(2,1)} %k.1, bf16[128,1024]{1,0:T(8,128)(2,1)} %v.1, bf16[128,1536]{1,0:T(8,128)(2,1)} %res.1, ...), custom_call_target="tpu_custom_call" | custom-call | tf_op jit(solution)/shard_map/layer/pallas_call | solution.py:326
  38.9 3.9 %finish.1 = (bf16[128,1536]{1,0:T(8,128)(2,1)}, bf16[128,6144]{1,0:T(8,128)(2,1)}) custom-call(bf16[128,1536]{1,0:T(8,128)(2,1)} %get-tuple-element.5.ns, bf16[12,128,512]{2,1,0:T(8,128)(2,1)} %get-tuple-element.6.hid, f32[128,128]{1,0:T(8,128)} %get-tuple-element.7.scale, f32[1,6144]{1,0:T(1,128)} %bitcast.2), custom_call_target="tpu_custom_call" | custom-call | tf_op jit(solution)/shard_map/finish/pallas_call | solution.py:365
